TPU v7x, 256 devices: a whole 4x4x8 slice. The times are simulated.
256 devices in a mesh: grp: 8 (over z), sub: 32 (over x, y, core).
Axes of the slice: x: 4, y: 4, z: 8, core: 2. Of those that a mesh axis runs over, the one named last changes fastest.
Arguments:
- residual: float32 [16, 98304], P(None, 'sub'), may hold values from -6 to 6
- margin: int32 [32, 8], replicated, may hold values from 0 to 767, as said below
- aggregate: int32 [768], P('sub'), may hold values from 0 to 63
- local_factor: bfloat16 [32, 4096, 4096], P('sub', 'grp'), may hold values from -0.09375 to 0.09375
- coarse_factor: bfloat16 [8192, 8192], P('sub'), may hold values from -0.0625 to 0.0625
Outputs:
- preconditioned: float32 [16, 98304], P('grp', 'sub')
Inputs may be any that keep to these rules, and one draw needn't show every extreme that they name: `margin`: for subdomain s, every entry names a block owned by another subdomain (block b is owned by subdomain b // 24); the entries of one row are distinct. Up to 8 entries of one row may name blocks of the same owner, and in every draw some row takes all of its entries from a single owner. `aggregate`: the counts of global blocks for each coarse block are whole numbers and may cross devices as int32.
All inputs are finite; a program needn't handle non-finite values.
Results may differ from a plain program's by a relative error of at most 0.0033.
Values sent between devices are 32-bit elements; how exact they have to be, the bound alone decides.
A program may use at most 64 MiB of HBM per device.

v0:
```python
import jax
import jax.numpy as jnp
from jax import lax
from jax.sharding import PartitionSpec as P

BLK = 128
NCB = 64


def row_of(table, index):
    return lax.dynamic_index_in_dim(table, index, 0, keepdims=False)


def on_device(residual, margin, aggregate, local_factor, coarse_factor):
    sub_count = lax.axis_size("sub")
    grp_count = lax.axis_size("grp")
    my_index = lax.axis_index("sub")
    grp_index = lax.axis_index("grp")
    rhs_count, own_width = residual.shape
    owned = own_width // BLK
    group_rows = rhs_count // grp_count
    blocks = residual.reshape(rhs_count, owned, BLK)
    exact = lax.Precision.HIGHEST
    my_list = row_of(margin, my_index)
    all_blocks = jnp.arange(owned * sub_count, dtype=jnp.int32)
    selector = (my_list[:, None] == all_blocks[None, :]).astype(jnp.float32)
    whole = lax.all_gather(blocks, "sub", axis=1, tiled=True)
    halo_rows = jnp.einsum("kb,rbc->rkc", selector, whole, precision=exact)
    local_rhs = (
        jnp.concatenate([blocks, halo_rows], axis=1).reshape(rhs_count, -1).astype(jnp.bfloat16)
    )
    factor = local_factor[0]
    inner_term = jnp.dot(local_rhs, factor.T, preferred_element_type=jnp.float32).astype(
        jnp.bfloat16
    )
    local_sol = lax.psum_scatter(
        jnp.dot(inner_term, factor, preferred_element_type=jnp.float32),
        "grp",
        scatter_dimension=0,
        tiled=True,
    )
    local_sol = local_sol.reshape(group_rows, -1, BLK)
    own_part = local_sol[:, :owned]
    back_rows = local_sol[:, owned:]
    spread = jnp.einsum("kb,rkc->rbc", selector, back_rows, precision=exact)
    returned = lax.psum_scatter(spread, "sub", scatter_dimension=1, tiled=True)
    catalog = jnp.arange(NCB, dtype=jnp.int32)
    member = (aggregate[:, None] == catalog[None, :]).astype(jnp.float32)
    mine = lax.dynamic_slice_in_dim(blocks, grp_index * group_rows, group_rows, 0)
    sums_part = jnp.einsum("rbk,bj->rjk", mine, member, precision=exact)
    sums, counts = lax.psum((sums_part, jnp.sum(member, axis=0)), "sub")
    coarse_rhs = (
        (sums / jnp.maximum(counts, 1.0)[None, :, None])
        .reshape(group_rows, -1)
        .astype(jnp.bfloat16)
    )
    inner_coarse = jnp.dot(coarse_rhs, coarse_factor.T, preferred_element_type=jnp.float32).astype(
        jnp.bfloat16
    )
    coarse_part = jnp.dot(inner_coarse, coarse_factor, preferred_element_type=jnp.float32)
    coarse_sol = lax.psum(coarse_part, "sub")
    prolonged = jnp.einsum(
        "rjk,bj->rbk", coarse_sol.reshape(group_rows, NCB, BLK), member, precision=exact
    )
    result = own_part + returned + prolonged
    return result.reshape(group_rows, -1)


def solution(mesh):
    placed = (P(None, "sub"), P(), P("sub"), P("sub", "grp", None), P("sub", None))
    return jax.shard_map(
        on_device, mesh=mesh, in_specs=placed, out_specs=P("grp", "sub"), check_vma=False
    )
```

profile of v0, /device:TPU:2, one launch (start us, length us, event | category | flops | bytes accessed | tf_op | source)
XLA Modules:
  0.0 460.0 jit_solution(2734043562929597561)
XLA Ops:
  6.5 1.0 copy.9
  7.5 1.6 convolution_bitcast_fusion.2
  9.2 0.7 all-gather.2.cloned.1.call-update
  10.0 0.2 dynamic-slice_reduce_fusion
  10.2 1.3 dynamic-slice
  12.1 0.7 convert_reduce_fusion
  12.8 55.4 %psum.22 = f32[64]{0:T(128)S(1)} all-reduce(f32[64]{0:T(128)S(1)} %convert_reduce_fusion), channel_id=1, replica_groups=mesh['grp'=8,'sub'=32] {'sub'}, use_global_device_ids=true, to_apply=%region_4.5 | all-reduce | flops 64 | bytes 512 | tf_op jit(solution)/shard_map/psum | solution.py:51
  68.3 0.9 bitcast_convert_fusion
  69.2 50.8 %all-reduce.5.cloned.1.call-done = f32[2,64,128]{2,1,0:T(8,128)} async-done(((f32[2,64,128]{2,1,0:T(8,128)}), f32[2,64,128]{2,1,0:T(8,128)}) %all-reduce.5.cloned.1.call-update) | async-done | bytes 65552 | tf_op jit(solution)/shard_map/psum | solution.py:51
  120.0 0.9 fusion.20
  120.9 54.7 %all-gather.2.cloned.1.call-done = f32[16,768,128]{2,1,0:T(8,128)} async-done(((f32[16,24,128]{2,1,0:T(8,128)}), f32[16,768,128]{2,1,0:T(8,128)}) %all-gather.2.cloned.1.call-update) | async-done | bytes 6291472 | tf_op jit(solution)/shard_map/all_gather | solution.py:27
  175.7 4.8 %fusion.4 = bf16[16,8,128]{2,1,0:T(8,128)(2,1)S(1)} fusion(f32[16,768,128]{2,1,0:T(8,128)} %all-gather.2.cloned.1.call-done, s32[8]{0:T(128)S(1)} %dynamic-slice_reduce_fusion), kind=kOutput, calls=%fused_computation.8 | convolution fusion | flops 151017472 | bytes 6324256 | tf_op jit(solution)/shard_map/kb,rbc->rkc/dot_general | solution.py:28
  180.5 6.0 %fusion = f32[16,4096]{1,0:T(8,128)} fusion(bf16[1,512,4096]{2,1,0:T(8,128)(2,1)} %param.8, bf16[2,8,32,128]{3,2,1,0:T(8,128)(2,1)S(1)} %bitcast.65), kind=kOutput, calls=%fused_computation | convolution fusion | flops 134225920 | bytes 4587520 | tf_op jit(solution)/shard_map/dot_general | solution.py:37
  186.6 0.0 all-reduce.7.cloned.1.call-start
  186.6 6.4 %convolution_bitcast_fusion.1 = f32[1,2,64,128]{3,1,2,0:T(2,128)S(1)} fusion(bf16[256,8192]{1,0:T(8,128)(2,1)} %param.9, bf16[1,2,64,128]{3,2,1,0:T(8,128)(2,1)S(1)} %fusion.20), kind=kOutput, calls=%fused_computation.5 | convolution fusion | flops 16777728 | bytes 4292608 | tf_op jit(solution)/shard_map/dot_general | solution.py:60
  193.0 0.6 copy.28
  193.6 0.0 reduce-scatter.2.cloned.1.call-start
  193.7 65.8 %all-reduce.9.cloned.1.call-done = f32[16,4096]{1,0:T(8,128)} async-done(((f32[16,4096]{1,0:T(8,128)}), f32[16,4096]{1,0:T(8,128)}) %all-reduce.9.cloned.1.call-update) | async-done | bytes 262160
  259.4 0.9 dynamic-slice_bitcast_fusion
  260.4 1.5 convolution_bitcast_fusion
  261.9 105.6 %all-reduce.7.cloned.1.call-done = f32[2,64,128]{2,1,0:T(8,128)} async-done(((f32[2,64,128]{2,1,0:T(8,128)}), f32[2,64,128]{2,1,0:T(8,128)}) %all-reduce.7.cloned.1.call-update) | async-done | bytes 65552 | tf_op jit(solution)/shard_map/psum | solution.py:61
  367.4 84.3 %reduce-scatter.2.cloned.1.call-done = f32[2,24,128]{2,1,0:T(8,128)} async-done(((f32[2,768,128]{2,1,0:T(8,128)}), f32[2,24,128]{2,1,0:T(8,128)}) %reduce-scatter.2.cloned.1.call-update) | async-done | bytes 24592 | tf_op jit(solution)/shard_map/reduce_scatter | solution.py:46
  451.8 1.0 fusion.11
  452.8 0.6 copy.30
  (16 shorter events, 0.2 us)
Async XLA Ops:
  6.5 3.5 copy-start
  6.5 113.4 %all-reduce.5.cloned.1.call-start = ((), (), s32[]{:S(2)}) async-start(), calls=%async_computation.3 | async-start | bytes 131072 | tf_op jit(solution)/shard_map/psum | solution.py:51
  7.5 1.7 copy-start.1
  9.2 166.5 %all-gather.2.cloned.1.call-start = ((), (), s32[]{:S(2)}) async-start(), calls=%async_computation.1 | async-start | bytes 6488064 | tf_op jit(solution)/shard_map/all_gather | solution.py:27
  9.9 249.5 %all-reduce.9.cloned.1.call-start = ((), (), s32[]{:S(2)}) async-start(), calls=%async_computation.5 | async-start | bytes 524288
  186.5 265.2 %copy-start.2 = (s32[24]{0:T(128)S(1)}, s32[24]{0:T(128)}, u32[]{:S(2)}) copy-start(s32[24]{0:T(128)} %param.7) | copy-start | bytes 292
  186.6 180.9 %all-reduce.7.cloned.1.call-start = ((), (), s32[]{:S(2)}) async-start(), calls=%async_computation.4 | async-start | bytes 131072 | tf_op jit(solution)/shard_map/psum | solution.py:61
  193.6 258.1 %reduce-scatter.2.cloned.1.call-start = ((), (), s32[]{:S(2)}) async-start(), calls=%async_computation.2 | async-start | bytes 811008 | tf_op jit(solution)/shard_map/reduce_scatter | solution.py:46
Sparse Core Ops, SparseCore 0:
  10.6 109.3 all-reduce.4
  122.7 52.9 all-gather.1
  186.7 72.7 all-reduce.8
  262.5 104.8 all-reduce.6
  371.1 80.6 reduce-scatter.1
where the time goes:
time: 460 us
  waiting for transfers between devices  362 us (79%)
  blocking collectives  55.4 us (12%)
  matrix products  21.3 us (5%)
  between operations  13.9 us (3%)
  local copies, waits for them, and re-layouts  4.62 us (1%)
    psum x1, waiting for transfers between devices, on_device(): coarse_sol = lax.psum(coarse_part, 'sub')  106 us
    reduce_scatter x1, waiting for transfers between devices, on_device(): returned = lax.psum_scatter(spread, 'sub', scatter_dimension=1, tiled=True)  84.3 us
    unnamed x6, waiting for transfers between devices  66.5 us
    psum x1, blocking collectives, on_device(): sums, counts = lax.psum((sums_part, jnp.sum(member, axis=0)), 'sub')  55.4 us
    all_gather x1, waiting for transfers between devices, on_device(): whole = lax.all_gather(blocks, 'sub', axis=1, tiled=True)  54.7 us
    psum x1, waiting for transfers between devices, on_device(): sums, counts = lax.psum((sums_part, jnp.sum(member, axis=0)), 'sub')  50.8 us
  transfers between devices with their start and end apart: 5, of which 5 were waited for; matrix products, arithmetic and copies ran while one was open for 3% of the time, Pallas kernels for 0%

commit v1 on v0

--- a/solution.py
+++ b/solution.py
@@ -5,6 +5,7 @@
 
 BLK = 128
 NCB = 64
+bring_the_steps_all = lambda mat, axis_tag: jnp.sum(lax.all_gather(mat, axis_name=axis_tag), 0)
 
 
 def row_of(table, index):
@@ -58,7 +59,7 @@
         jnp.bfloat16
     )
     coarse_part = jnp.dot(inner_coarse, coarse_factor, preferred_element_type=jnp.float32)
-    coarse_sol = lax.psum(coarse_part, "sub")
+    coarse_sol = bring_the_steps_all(coarse_part, "sub")
     prolonged = jnp.einsum(
         "rjk,bj->rbk", coarse_sol.reshape(group_rows, NCB, BLK), member, precision=exact
     )

time: 460 us -> 402 us (0.87)
  waiting for transfers between devices: 362 us -> 302 us
    psum x1 -> x0, waiting for transfers between devices: 106 us -> none  [on_device(): coarse_sol = lax.psum(coarse_part, 'sub')]
    all_gather x0 -> x1, waiting for transfers between devices: none -> 46.7 us  [lax.all_gather(mat, axis_name=axis_tag)]
  transfers between devices with their start and end apart: 5 -> 5, of which waited for: 5 -> 5; matrix products, arithmetic and copies ran while one was open for 3% -> 4% of each run, Pallas kernels for 0% -> 0%
where the time goes in v1:
time: 402 us; the launch traced here: 401 us
  waiting for transfers between devices  302 us (75%)
  blocking collectives  55.4 us (14%)
  matrix products  21.9 us (5%)
  between operations  13.9 us (3%)
  other arithmetic  4.9 us (1%)
    reduce_scatter x1, waiting for transfers between devices, on_device(): returned = lax.psum_scatter(spread, 'sub', scatter_dimension=1, tiled=True)  82.2 us
    unnamed x6, waiting for transfers between devices  65.3 us
    psum x1, blocking collectives, on_device(): sums, counts = lax.psum((sums_part, jnp.sum(member, axis=0)), 'sub')  55.4 us
    all_gather x1, waiting for transfers between devices, on_device(): whole = lax.all_gather(blocks, 'sub', axis=1, tiled=True)  54.7 us
    psum x1, waiting for transfers between devices, on_device(): sums, counts = lax.psum((sums_part, jnp.sum(member, axis=0)), 'sub')  52.7 us
    all_gather x1, waiting for transfers between devices, lax.all_gather(mat, axis_name=axis_tag)  46.7 us
  transfers between devices with their start and end apart: 5, of which 5 were waited for; matrix products, arithmetic and copies ran while one was open for 4% of the time, Pallas kernels for 0%

profile of v1, /device:TPU:2, one launch (start us, length us, event | category | flops | bytes accessed | tf_op | source)
XLA Modules:
  0.0 401.2 jit_solution(14877120524996691215)
XLA Ops:
  6.5 1.0 copy.9
  7.5 1.6 convolution_bitcast_fusion.2
  9.2 0.7 all-gather.5.cloned.1.call-update
  10.0 0.2 dynamic-slice_reduce_fusion
  10.2 0.7 convert_reduce_fusion
  10.9 55.4 %psum.15 = f32[64]{0:T(128)S(1)} all-reduce(f32[64]{0:T(128)S(1)} %convert_reduce_fusion), channel_id=1, replica_groups=mesh['grp'=8,'sub'=32] {'sub'}, use_global_device_ids=true, to_apply=%region_4.5 | all-reduce | flops 64 | bytes 512 | tf_op jit(solution)/shard_map/psum | solution.py:52
  66.3 0.9 bitcast_convert_fusion
  67.3 52.7 %all-reduce.4.cloned.1.call-done = f32[2,64,128]{2,1,0:T(8,128)} async-done(((f32[2,64,128]{2,1,0:T(8,128)}), f32[2,64,128]{2,1,0:T(8,128)}) %all-reduce.4.cloned.1.call-update) | async-done | bytes 65552 | tf_op jit(solution)/shard_map/psum | solution.py:52
  120.0 0.9 fusion.22
  120.9 54.7 %all-gather.5.cloned.1.call-done = f32[16,768,128]{2,1,0:T(8,128)} async-done(((f32[16,24,128]{2,1,0:T(8,128)}), f32[16,768,128]{2,1,0:T(8,128)}) %all-gather.5.cloned.1.call-update) | async-done | bytes 6291472 | tf_op jit(solution)/shard_map/all_gather | solution.py:28
  175.7 4.8 %fusion.4 = bf16[16,8,128]{2,1,0:T(8,128)(2,1)S(1)} fusion(f32[16,768,128]{2,1,0:T(8,128)} %all-gather.5.cloned.1.call-done, s32[8]{0:T(128)S(1)} %dynamic-slice_reduce_fusion), kind=kOutput, calls=%fused_computation.8 | convolution fusion | flops 151017472 | bytes 6324256 | tf_op jit(solution)/shard_map/kb,rbc->rkc/dot_general | solution.py:29
  180.5 6.0 %fusion = f32[16,4096]{1,0:T(8,128)} fusion(bf16[1,512,4096]{2,1,0:T(8,128)(2,1)} %param.8, bf16[2,8,32,128]{3,2,1,0:T(8,128)(2,1)S(1)} %bitcast.65), kind=kOutput, calls=%fused_computation.1 | convolution fusion | flops 134225920 | bytes 4587520 | tf_op jit(solution)/shard_map/dot_general | solution.py:38
  186.6 0.0 all-gather.7.cloned.1.call-start
  186.6 7.0 %convolution_bitcast_fusion = f32[1,2,8192]{2,1,0:T(2,128)} fusion(bf16[256,8192]{1,0:T(8,128)(2,1)} %param.9, bf16[1,2,64,128]{3,2,1,0:T(8,128)(2,1)S(1)} %fusion.22), kind=kOutput, calls=%fused_computation | convolution fusion | flops 16777728 | bytes 4292608 | tf_op jit(solution)/shard_map/dot_general | solution.py:61
  193.6 0.0 reduce-scatter.2.cloned.1.call-start
  193.7 0.6 dynamic-slice
  194.9 64.5 %all-reduce.6.cloned.1.call-done = f32[16,4096]{1,0:T(8,128)} async-done(((f32[16,4096]{1,0:T(8,128)}), f32[16,4096]{1,0:T(8,128)}) %all-reduce.6.cloned.1.call-update) | async-done | bytes 262160
  259.4 0.9 dynamic-slice_bitcast_fusion
  260.4 1.5 convolution_bitcast_fusion.1
  261.9 46.7 %all-gather.7.cloned.1.call-done = f32[32,2,8192]{2,1,0:T(2,128)} async-done(((f32[1,2,8192]{2,1,0:T(2,128)}), f32[32,2,8192]{2,1,0:T(2,128)}) %all-gather.7.cloned.1.call-update) | async-done | bytes 2097168 | tf_op jit(solution)/shard_map/all_gather | solution.py:8
  308.6 2.3 reduce_sum.19
  310.9 82.2 %reduce-scatter.2.cloned.1.call-done = f32[2,24,128]{2,1,0:T(8,128)} async-done(((f32[2,768,128]{2,1,0:T(8,128)}), f32[2,24,128]{2,1,0:T(8,128)}) %reduce-scatter.2.cloned.1.call-update) | async-done | bytes 24592 | tf_op jit(solution)/shard_map/reduce_scatter | solution.py:47
  393.1 0.9 fusion.11
  394.0 0.6 copy.32
  (18 shorter events, 0.2 us)
Async XLA Ops:
  6.5 3.4 copy-start
  6.5 113.4 %all-reduce.4.cloned.1.call-start = ((), (), s32[]{:S(2)}) async-start(), calls=%async_computation.3 | async-start | bytes 131072 | tf_op jit(solution)/shard_map/psum | solution.py:52
  7.5 1.7 copy-start.1
  9.2 166.5 %all-gather.5.cloned.1.call-start = ((), (), s32[]{:S(2)}) async-start(), calls=%async_computation.1 | async-start | bytes 6488064 | tf_op jit(solution)/shard_map/all_gather | solution.py:28
  9.9 249.5 %all-reduce.6.cloned.1.call-start = ((), (), s32[]{:S(2)}) async-start(), calls=%async_computation.5 | async-start | bytes 524288
  186.5 7.1 %copy-start.3 = (u32[256]{0:T(256)S(1)}, u32[256]{0:T(256)}, u32[]{:S(2)}) copy-start(u32[256]{0:T(256)} %constant.28) | copy-start | bytes 3076
  186.6 206.5 %copy-start.2 = (s32[24]{0:T(128)S(1)}, s32[24]{0:T(128)}, u32[]{:S(2)}) copy-start(s32[24]{0:T(128)} %param.7) | copy-start | bytes 292
  186.6 122.0 %all-gather.7.cloned.1.call-start = ((), (), s32[]{:S(2)}) async-start(), calls=%async_computation.4 | async-start | bytes 2162688 | tf_op jit(solution)/shard_map/all_gather | solution.py:8
  193.6 199.5 %reduce-scatter.2.cloned.1.call-start = ((), (), s32[]{:S(2)}) async-start(), calls=%async_computation.2 | async-start | bytes 811008 | tf_op jit(solution)/shard_map/reduce_scatter | solution.py:47
Sparse Core Ops, SparseCore 0:
  10.6 109.3 all-reduce.3
  122.7 52.9 all-gather.4
  186.7 72.7 all-reduce.5
  261.8 46.7 all-gather.6
  312.2 80.7 reduce-scatter.1
